TPU v7x, 512 devices: a whole 4x8x8 slice. The times are simulated.
512 devices in a mesh: curve: 64 (over z, x, core), split: 8 (over y).
Axes of the slice: x: 4, y: 8, z: 8, core: 2. Of those that a mesh axis runs over, the one named last changes fastest.
Arguments:
- rhs_load: float32 [8192, 512], P(('curve', 'split')), may hold values from -6 to 6
- stretch: float32 [3, 8192], P(None, ('curve', 'split')), may hold values from 0.5 to 4
- helm_shift: float32 [8192], P(('curve', 'split')), may hold values from 100 to 1000
- local_slot: int32 [8192, 512], P(('curve', 'split')), may hold values from 0 to 5487, as said below
- share_curve: int32 [64, 8, 4, 128], P('curve', 'split'), may hold values from 0 to 5488, as said below
- share_split: int32 [64, 8, 2, 128], P('curve', 'split'), may hold values from 0 to 5488, as said below
- coarse_slot: int32 [8, 8192], P(None, ('curve', 'split')), may hold values from 0 to 15
- x_vals: float32 [16, 8192], P(None, ('curve', 'split')), may hold values from -4 to 4
- x_cols: int32 [16, 8192], P(None, ('curve', 'split')), may hold values from 0 to 8191, as said below
- x_count: int32 [8192], P(('curve', 'split')), may hold values from 1 to 16, as said below
Outputs:
- solution: float32 [8192, 512], P(('curve', 'split'))
- residual: float32 [8192, 512], P(('curve', 'split'))
Inputs may be any that keep to these rules, and one draw needn't show every extreme that they name: `local_slot`: every slot 0 to 5487 of a device's node vector is named by one or more of its points. `share_curve`: each entry is a node slot of the device, or 5488 for an empty entry; the slots of one list are distinct; the list of device (c, s) for offset o and the partner's list for offset -o name shared nodes entry by entry and have equal numbers of filled entries, which come first; lists towards partitions that do not exist are empty; some list is full in every draw. `share_split`: as for share_curve, with partner (c, s + o) for the offsets -1 and 1. `x_cols`: entry 0 of row i is i; entries 1 to 7 lie within 32 of i; the later entries lie among the coarse unknowns of separator devices of a nested dissection of the device numbers, one level an entry. `x_count`: some rows use all 16 entries.
All inputs are finite; a program needn't handle non-finite values.
Results may differ from a plain program's by a relative error of at most 0.0009.
Values sent between devices are 32-bit elements; how exact they have to be, the bound alone decides.
No kernel may reach another device: no remote copies, remote signals or barrier semaphores. Data moves between devices by JAX's collectives and lax.ppermute only.
A program may use at most 64 MiB of HBM per device.

v0:
```python
import jax
import jax.numpy as jnp
import numpy as np
from jax import lax
from jax.sharding import PartitionSpec as P

ITERS = 4


def from_behind(block, axis, distance):
    devices = range(lax.axis_size(axis))
    route = [(i - distance, i) for i in devices if i - distance in devices]
    return lax.ppermute(block, axis, route)


def element_tables():
    poly_order = 7
    node_count = poly_order + 1
    gll_nodes = -np.cos(np.pi * np.arange(node_count) / poly_order)
    legendre = np.zeros((node_count, node_count))
    for sweep in range(60):
        legendre[:, 0] = 1.0
        legendre[:, 1] = gll_nodes
        for degree in range(2, node_count):
            legendre[:, degree] = (
                (2 * degree - 1) * gll_nodes * legendre[:, degree - 1]
                - (degree - 1) * legendre[:, degree - 2]
            ) / degree
        gll_nodes = gll_nodes - (
            gll_nodes * legendre[:, poly_order] - legendre[:, poly_order - 1]
        ) / (node_count * legendre[:, poly_order])
    for degree in range(2, node_count):
        legendre[:, degree] = (
            (2 * degree - 1) * gll_nodes * legendre[:, degree - 1]
            - (degree - 1) * legendre[:, degree - 2]
        ) / degree
    top_poly = legendre[:, poly_order]
    quad_weights = 2.0 / (poly_order * node_count * top_poly * top_poly)
    deriv_matrix = np.zeros((node_count, node_count))
    for row_index in range(node_count):
        for col_index in range(node_count):
            if row_index != col_index:
                deriv_matrix[row_index, col_index] = top_poly[row_index] / (
                    top_poly[col_index] * (gll_nodes[row_index] - gll_nodes[col_index])
                )
    deriv_matrix[0, 0] = -poly_order * node_count / 4.0
    deriv_matrix[poly_order, poly_order] = poly_order * node_count / 4.0
    identity = np.eye(node_count)
    mass_diag = (
        quad_weights[:, None, None] * quad_weights[None, :, None] * quad_weights[None, None, :]
    ).reshape(-1)
    stiff_list = []
    for deriv_kron in (
        np.kron(np.kron(deriv_matrix, identity), identity),
        np.kron(np.kron(identity, deriv_matrix), identity),
        np.kron(identity, np.kron(identity, deriv_matrix)),
    ):
        stiff_list.append(deriv_kron.T @ (mass_diag[:, None] * deriv_kron))
    stiffness = np.concatenate(stiff_list, axis=1)
    diag_index = np.arange(stiff_list[0].shape[0])
    stiff_diag = np.stack([block[diag_index, diag_index] for block in stiff_list])
    hat_values = np.stack([(1.0 - gll_nodes) / 2.0, (1.0 + gll_nodes) / 2.0])
    coarse_table = (
        hat_values[:, None, None, :, None, None]
        * hat_values[None, :, None, None, :, None]
        * hat_values[None, None, :, None, None, :]
    ).reshape(8, -1)
    return (mass_diag, stiffness, stiff_diag, coarse_table)


def local_operator(element_field, stiffness, mass_diag, stretch, helm_shift):
    products = jnp.dot(
        element_field,
        stiffness,
        precision=lax.Precision.HIGHEST,
        preferred_element_type=jnp.float32,
    )
    point_count = element_field.shape[1]
    result = stretch[0][:, None] * products[:, :point_count]
    result = result + stretch[1][:, None] * products[:, point_count : 2 * point_count]
    result = result + stretch[2][:, None] * products[:, 2 * point_count :]
    return result + helm_shift[:, None] * mass_diag[None, :] * element_field


def assemble(fields, point_slots, curve_lists, split_lists, node_count):
    batch_count = fields.shape[0]
    flattened = fields.reshape(batch_count, -1)
    node_sums = jax.vmap(
        lambda values: jax.ops.segment_sum(values, point_slots, num_segments=node_count + 1)
    )(flattened)
    assembled = node_sums
    for list_index, offset in enumerate((-1, 1)):
        outgoing = node_sums[:, split_lists[1 - list_index]]
        incoming = from_behind(outgoing, "split", -offset)
        assembled = assembled.at[:, split_lists[list_index]].add(incoming)
    reach = curve_lists.shape[0] // 2
    curve_offsets = list(range(-reach, 0)) + list(range(1, reach + 1))
    for list_index, offset in enumerate(curve_offsets):
        outgoing = node_sums[:, curve_lists[2 * reach - 1 - list_index]]
        incoming = from_behind(outgoing, "curve", -offset)
        assembled = assembled.at[:, curve_lists[list_index]].add(incoming)
    return assembled[:, point_slots].reshape(fields.shape)


def local(
    rhs_load,
    stretch,
    helm_shift,
    local_slot,
    share_curve,
    share_split,
    coarse_slot,
    x_vals,
    x_cols,
    x_count,
):
    mass_np, stiff_np, sdiag_np, coarse_np = element_tables()
    mass_diag = jnp.asarray(mass_np, dtype=jnp.float32)
    stiffness = jnp.asarray(stiff_np, dtype=jnp.float32)
    stiff_diag = jnp.asarray(sdiag_np, dtype=jnp.float32)
    coarse_table = jnp.asarray(coarse_np, dtype=jnp.float32)
    element_count = rhs_load.shape[0]
    node_count = 343 * element_count
    point_slots = local_slot.reshape(-1)
    curve_lists = share_curve.reshape(share_curve.shape[2], share_curve.shape[3])
    split_lists = share_split.reshape(share_split.shape[2], share_split.shape[3])
    coarse_rows = x_vals.shape[1]
    total_coarse = coarse_rows * lax.axis_size("curve") * lax.axis_size("split")
    diag_local = (
        stretch[0][:, None] * stiff_diag[0][None, :] + stretch[1][:, None] * stiff_diag[1][None, :]
    )
    diag_local = (
        diag_local
        + stretch[2][:, None] * stiff_diag[2][None, :]
        + helm_shift[:, None] * mass_diag[None, :]
    )
    setup = assemble(
        jnp.stack([jnp.ones_like(rhs_load), diag_local, rhs_load]),
        point_slots,
        curve_lists,
        split_lists,
        node_count,
    )
    multiplicity = setup[0]
    diag_a = setup[1]
    right = setup[2]
    live_entry = jnp.arange(x_vals.shape[0])[:, None] < x_count[None, :]
    factor = jnp.where(live_entry, x_vals, jnp.zeros_like(x_vals))

    def global_dot(left_field, right_field):
        return lax.psum(jnp.sum(left_field * right_field / multiplicity), ("curve", "split"))

    def coarse_partial(scaled):
        restricted = lax.dot_general(
            coarse_table,
            scaled,
            (((1,), (1,)), ((), ())),
            precision=lax.Precision.HIGHEST,
            preferred_element_type=jnp.float32,
        )
        loads = jax.ops.segment_sum(
            restricted.reshape(-1), coarse_slot.reshape(-1), num_segments=coarse_rows
        )
        return jax.ops.segment_sum(
            (factor * loads[None, :]).reshape(-1), x_cols.reshape(-1), num_segments=total_coarse
        )

    def coarse_correction(coarse_image):
        coarse_values = jnp.sum(factor * coarse_image[x_cols], axis=0)
        vertex_values = coarse_values[coarse_slot]
        return lax.dot_general(
            vertex_values,
            coarse_table,
            (((0,), (0,)), ((), ())),
            precision=lax.Precision.HIGHEST,
            preferred_element_type=jnp.float32,
        )

    def precondition(residual_field):
        scaled = residual_field / multiplicity
        partial_image = coarse_partial(scaled)
        jacobi_part = residual_field / diag_a
        coarse_image = lax.psum(partial_image, ("curve", "split"))
        precond_field = jacobi_part + coarse_correction(coarse_image)
        precond_norm = global_dot(residual_field, precond_field)
        return (precond_field, precond_norm)

    solution = jnp.zeros_like(rhs_load)
    residual = right
    precond, rz_value = precondition(residual)
    direction = precond
    for iteration in range(ITERS):
        image = assemble(
            local_operator(direction, stiffness, mass_diag, stretch, helm_shift)[None],
            point_slots,
            curve_lists,
            split_lists,
            node_count,
        )[0]
        step_size = rz_value / global_dot(direction, image)
        solution = solution + step_size * direction
        residual = residual - step_size * image
        if iteration < ITERS - 1:
            precond, rz_next = precondition(residual)
            direction = precond + rz_next / rz_value * direction
            rz_value = rz_next
    return (solution, residual)


def solution(mesh):
    in_specs = (
        P(("curve", "split"), None),
        P(None, ("curve", "split")),
        P(("curve", "split")),
        P(("curve", "split"), None),
        P("curve", "split", None, None),
        P("curve", "split", None, None),
        P(None, ("curve", "split")),
        P(None, ("curve", "split")),
        P(None, ("curve", "split")),
        P(("curve", "split")),
    )
    out_specs = (P(("curve", "split"), None), P(("curve", "split"), None))
    return jax.shard_map(local, mesh=mesh, in_specs=in_specs, out_specs=out_specs, check_vma=False)
```

profile of v0, /device:TPU:27, one launch (start us, length us, event | category | flops | bytes accessed | tf_op | source)
XLA Modules:
  0.0 1746.6 jit_solution(16968491514519512765)
XLA Ops:
  6.5 2.6 copy.18
  9.2 45.0 %scatter_custom_fusion = f32[3,5489]{0,1:T(8,128)S(1)} fusion(s32[8192]{0:T(1024)S(1)} %bitcast.195, f32[8192,3]{1,0:T(8,128)} %copy.18, f32[]{:T(128)} %constant.10.clone.1), kind=kCustom, calls=%fused_computation.89 | custom fusion | flops 24576 | bytes 66380 | tf_op jit(solution)/shard_map/vmap()/scatter-add | solution.py:89
  55.4 4.4 collective-permute-start
  63.7 3.1 collective-permute-start.2
  67.4 3.9 collective-permute-start.3
  76.1 2.5 collective-permute-start.5
  78.8 2.3 scatter_custom_fusion.1
  81.0 2.4 scatter_custom_fusion.2
  83.5 2.3 scatter_custom_fusion.3
  85.7 2.3 scatter_custom_fusion.4
  88.0 2.3 scatter_custom_fusion.5
  90.4 2.7 scatter_custom_fusion.6
  93.1 27.7 %gather_fusion.6 = f32[8192,3]{1,0:T(8,128)} fusion(f32[3,5489]{0,1:T(8,128)S(1)} %scatter_custom_fusion.6, s32[8192]{0:T(1024)S(1)} %broadcast_clamp_fusion), kind=kCustom, calls=%fused_computation.6 | custom fusion | bytes 229376 | tf_op jit(solution)/shard_map/gather | solution.py:102
  120.8 10.2 slice_reduce_fusion.1
  132.8 2.3 scatter_custom_fusion.8
  135.2 106.3 %psum.84 = f32[8192]{0:T(1024)S(1)} all-reduce(f32[8192]{0:T(1024)S(1)} %scatter_custom_fusion.8), channel_id=1, replica_groups=mesh['curve'=64,'split'=8] {'curve','split'}, use_global_device_ids=true, to_apply=%region_9.10 | all-reduce | flops 8192 | bytes 65536 | tf_op jit(solution)/shard_map/psum | solution.py:183
  246.8 43.4 %scatter_custom_fusion.9 = f32[5489]{0:T(1024)S(1)} fusion(s32[8192]{0:T(1024)S(1)} %bitcast.196, f32[8192]{0:T(1024)S(1)} %bitcast.201, f32[]{:T(128)} %constant.10.clone.1), kind=kCustom, calls=%fused_computation.198 | custom fusion | flops 8192 | bytes 21960 | tf_op jit(solution)/shard_map/vmap()/scatter-add | solution.py:89
  295.3 2.4 collective-permute-start.6
  300.2 2.9 collective-permute-start.7
  305.1 4.2 collective-permute-start.9
  311.2 2.2 collective-permute-start.11
  321.4 45.5 %gather_fusion.15 = f32[8192]{0:T(1024)S(1)} fusion(f32[5489]{0:T(1024)S(1)} %scatter_fusion.5, s32[8192]{0:T(1024)S(1)} %broadcast_clamp_fusion), kind=kCustom, calls=%fused_computation.15 | custom fusion | bytes 98304 | tf_op jit(solution)/shard_map/gather | solution.py:102
  367.6 100.7 %all-reduce = (f32[]{:T(128)}, f32[]{:T(128)}) all-reduce(f32[]{:T(128)} %get-tuple-element.6, f32[]{:T(128)} %get-tuple-element.5), channel_id=1, replica_groups=mesh['curve'=64,'split'=8] {'curve','split'}, use_global_device_ids=true, to_apply=%region_12.13 | all-reduce | flops 2 | bytes 16 | tf_op jit(solution)/shard_map/psum | solution.py:151
  471.6 2.5 scatter_custom_fusion.17
  474.1 94.6 %psum.87 = f32[8192]{0:T(1024)S(1)} all-reduce(f32[8192]{0:T(1024)S(1)} %scatter_custom_fusion.17), channel_id=1, replica_groups=mesh['curve'=64,'split'=8] {'curve','split'}, use_global_device_ids=true, to_apply=%region_24.25 | all-reduce | flops 8192 | bytes 65536 | tf_op jit(solution)/shard_map/psum | solution.py:183
  572.7 96.4 %psum.88 = f32[]{:T(128)} all-reduce(f32[]{:T(128)} %get-tuple-element.18), channel_id=1, replica_groups=mesh['curve'=64,'split'=8] {'curve','split'}, use_global_device_ids=true, to_apply=%region_27.28 | all-reduce | flops 1 | bytes 8 | tf_op jit(solution)/shard_map/psum | solution.py:151
  672.1 43.2 %scatter_custom_fusion.18 = f32[5489]{0:T(1024)S(1)} fusion(s32[8192]{0:T(1024)S(1)} %bitcast.197, f32[8192]{0:T(1024)S(1)} %bitcast.202, f32[]{:T(128)} %constant.10.clone.1), kind=kCustom, calls=%fused_computation.196 | custom fusion | flops 8192 | bytes 21960 | tf_op jit(solution)/shard_map/vmap()/scatter-add | solution.py:89
  725.2 3.1 collective-permute-start.13
  730.2 3.7 collective-permute-start.15
  735.9 2.2 collective-permute-start.17
  746.1 45.5 %gather_fusion.24 = f32[8192]{0:T(1024)S(1)} fusion(f32[5489]{0:T(1024)S(1)} %scatter_fusion.11, s32[8192]{0:T(1024)S(1)} %broadcast_clamp_fusion), kind=kCustom, calls=%fused_computation.24 | custom fusion | bytes 98304 | tf_op jit(solution)/shard_map/gather | solution.py:102
  792.3 101.2 %psum.89 = f32[]{:T(128)} all-reduce(f32[]{:T(128)} %fusion.33), channel_id=1, replica_groups=mesh['curve'=64,'split'=8] {'curve','split'}, use_global_device_ids=true, to_apply=%region_36.37 | all-reduce | flops 1 | bytes 8 | tf_op jit(solution)/shard_map/psum | solution.py:151
  897.1 2.5 scatter_custom_fusion.26
  899.6 94.6 %psum.90 = f32[8192]{0:T(1024)S(1)} all-reduce(f32[8192]{0:T(1024)S(1)} %scatter_custom_fusion.26), channel_id=1, replica_groups=mesh['curve'=64,'split'=8] {'curve','split'}, use_global_device_ids=true, to_apply=%region_39.40 | all-reduce | flops 8192 | bytes 65536 | tf_op jit(solution)/shard_map/psum | solution.py:183
  998.2 96.3 %psum.91 = f32[]{:T(128)} all-reduce(f32[]{:T(128)} %get-tuple-element.20), channel_id=1, replica_groups=mesh['curve'=64,'split'=8] {'curve','split'}, use_global_device_ids=true, to_apply=%region_42.43 | all-reduce | flops 1 | bytes 8 | tf_op jit(solution)/shard_map/psum | solution.py:151
  1097.6 43.2 %scatter_custom_fusion.27 = f32[5489]{0:T(1024)S(1)} fusion(s32[8192]{0:T(1024)S(1)} %bitcast.198, f32[8192]{0:T(1024)S(1)} %bitcast.203, f32[]{:T(128)} %constant.10.clone.1), kind=kCustom, calls=%fused_computation.194 | custom fusion | flops 8192 | bytes 21960 | tf_op jit(solution)/shard_map/vmap()/scatter-add | solution.py:89
  1150.6 3.1 collective-permute-start.19
  1155.7 3.6 collective-permute-start.21
  1171.6 45.5 %gather_fusion.33 = f32[8192]{0:T(1024)S(1)} fusion(f32[5489]{0:T(1024)S(1)} %scatter_fusion.17, s32[8192]{0:T(1024)S(1)} %broadcast_clamp_fusion), kind=kCustom, calls=%fused_computation.33 | custom fusion | bytes 98304 | tf_op jit(solution)/shard_map/gather | solution.py:102
  1217.8 101.1 %psum.92 = f32[]{:T(128)} all-reduce(f32[]{:T(128)} %fusion.35), channel_id=1, replica_groups=mesh['curve'=64,'split'=8] {'curve','split'}, use_global_device_ids=true, to_apply=%region_51.52 | all-reduce | flops 1 | bytes 8 | tf_op jit(solution)/shard_map/psum | solution.py:151
  1322.1 2.5 scatter_custom_fusion.35
  1324.6 94.6 %psum.93 = f32[8192]{0:T(1024)S(1)} all-reduce(f32[8192]{0:T(1024)S(1)} %scatter_custom_fusion.35), channel_id=1, replica_groups=mesh['curve'=64,'split'=8] {'curve','split'}, use_global_device_ids=true, to_apply=%region_54.55 | all-reduce | flops 8192 | bytes 65536 | tf_op jit(solution)/shard_map/psum | solution.py:183
  1423.2 96.2 %psum.94 = f32[]{:T(128)} all-reduce(f32[]{:T(128)} %get-tuple-element.22), channel_id=1, replica_groups=mesh['curve'=64,'split'=8] {'curve','split'}, use_global_device_ids=true, to_apply=%region_57.58 | all-reduce | flops 1 | bytes 8 | tf_op jit(solution)/shard_map/psum | solution.py:151
  1522.4 43.2 %scatter_custom_fusion.36 = f32[5489]{0:T(1024)S(1)} fusion(s32[8192]{0:T(1024)S(1)} %bitcast.199, f32[8192]{0:T(1024)S(1)} %bitcast.200, f32[]{:T(128)} %constant.10.clone.1), kind=kCustom, calls=%fused_computation.192 | custom fusion | flops 8192 | bytes 21960 | tf_op jit(solution)/shard_map/vmap()/scatter-add | solution.py:89
  1575.5 3.1 collective-permute-start.25
  1580.5 3.7 collective-permute-start.27
  1596.6 45.5 %gather_fusion.42 = f32[8192]{0:T(1024)S(1)} fusion(f32[5489]{0:T(1024)S(1)} %scatter_fusion.23, s32[8192]{0:T(1024)S(1)} %broadcast_clamp_fusion), kind=kCustom, calls=%fused_computation.42 | custom fusion | bytes 98304 | tf_op jit(solution)/shard_map/gather | solution.py:102
  1642.8 101.1 %psum.95 = f32[]{:T(128)} all-reduce(f32[]{:T(128)} %fusion.37), channel_id=1, replica_groups=mesh['curve'=64,'split'=8] {'curve','split'}, use_global_device_ids=true, to_apply=%region_66.67 | all-reduce | flops 1 | bytes 8 | tf_op jit(solution)/shard_map/psum | solution.py:151
  (265 shorter events, 138.9 us)
Async XLA Ops:
  1.4 1096.0 %copy-start.6 = (f32[16]{0:T(128)}, f32[16]{0:T(128)S(1)}, u32[]{:S(2)}) copy-start(f32[16]{0:T(128)S(1)} %get-tuple-element.13) | copy-start | bytes 196
  1.4 1096.0 %copy-start.8 = (f32[16]{0:T(128)}, f32[16]{0:T(128)S(1)}, u32[]{:S(2)}) copy-start(f32[16]{0:T(128)S(1)} %get-tuple-element.14) | copy-start | bytes 196
  1.4 1096.0 %copy-start.10 = (f32[16]{0:T(128)}, f32[16]{0:T(128)S(1)}, u32[]{:S(2)}) copy-start(f32[16]{0:T(128)S(1)} %get-tuple-element.15) | copy-start | bytes 196
  6.4 56.0 %copy-start.23 = (s32[1,1,4,128]{3,2,1,0:T(4,128)S(1)}, s32[1,1,4,128]{3,2,1,0:T(4,128)}, u32[]{:S(2)}) copy-start(s32[1,1,4,128]{3,2,1,0:T(4,128)} %param.18) | copy-start | bytes 6148
  6.4 68.2 %copy-start.5 = (s32[16,16]{1,0:T(8,128)S(1)}, s32[16,16]{1,0:T(8,128)}, u32[]{:S(2)}) copy-start(s32[16,16]{1,0:T(8,128)} %param.22) | copy-start | bytes 3076
  6.5 68.3 %copy-start.12 = (s32[8,16]{1,0:T(8,128)S(1)}, s32[8,16]{1,0:T(8,128)}, u32[]{:S(2)}) copy-start(s32[8,16]{1,0:T(8,128)} %param.20) | copy-start | bytes 1540
  9.1 65.6 %copy-start.17 = (s32[1024]{0:T(1024)}, s32[1024]{0:T(1024)S(1)}, u32[]{:S(2)}) copy-start(s32[1024]{0:T(1024)S(1)} %get-tuple-element.26) | copy-start | bytes 12292
  9.1 81.2 %copy-start.18 = (s32[1024]{0:T(1024)}, s32[1024]{0:T(1024)S(1)}, u32[]{:S(2)}) copy-start(s32[1024]{0:T(1024)S(1)} %get-tuple-element.27) | copy-start | bytes 12292
  55.4 20.7 %collective-permute-start = (f32[3,128]{0,1:T(8,128)}, f32[3,128]{0,1:T(8,128)S(1)}, u32[]{:S(2)}, u32[]{:S(2)}) collective-permute-start(f32[3,128]{0,1:T(8,128)} %bitcast.8), channel_id=1, source_target_pairs={{0,1},{1,2},{2,3},{3,4},{4,5},{5,6},{6,7},{8,9},{9,10},{10,11},{11... | collective-permute-start | bytes 4616 | tf_op jit(solution)/shard_map/ppermute | solution.py:13
  60.5 20.6 %collective-permute-start.1 = (f32[3,128]{0,1:T(8,128)S(1)}, f32[3,128]{0,1:T(8,128)S(1)}, u32[]{:S(2)}, u32[]{:S(2)}) collective-permute-start(f32[3,128]{0,1:T(8,128)S(1)} %bitcast.252), channel_id=1, source_target_pairs={{1,0},{2,1},{3,2},{4,3},{5,4},{6,5},{7,6},{9,8},{10,9},{11,10},{12... | collective-permute-start | bytes 4616 | tf_op jit(solution)/shard_map/ppermute | solution.py:13
  62.4 21.0 %copy-start.19 = (s32[1024]{0:T(1024)}, s32[1024]{0:T(1024)S(1)}, u32[]{:S(2)}) copy-start(s32[1024]{0:T(1024)S(1)} %get-tuple-element.30) | copy-start | bytes 12292
  62.4 21.0 %copy-start.20 = (s32[1024]{0:T(1024)}, s32[1024]{0:T(1024)S(1)}, u32[]{:S(2)}) copy-start(s32[1024]{0:T(1024)S(1)} %get-tuple-element.31) | copy-start | bytes 12292
  63.7 19.8 %collective-permute-start.2 = (f32[3,128]{0,1:T(8,128)}, f32[3,128]{0,1:T(8,128)S(1)}, u32[]{:S(2)}, u32[]{:S(2)}) collective-permute-start(f32[3,128]{0,1:T(8,128)} %bitcast.16), channel_id=1, source_target_pairs={{0,16},{8,24},{16,32},{24,40},{32,48},{40,56},{48,64},{56,72},{64,... | collective-permute-start | bytes 4616 | tf_op jit(solution)/shard_map/ppermute | solution.py:13
  67.4 18.3 %collective-permute-start.3 = (f32[3,128]{0,1:T(8,128)S(1)}, f32[3,128]{0,1:T(8,128)S(1)}, u32[]{:S(2)}, u32[]{:S(2)}) collective-permute-start(f32[3,128]{0,1:T(8,128)S(1)} %bitcast.253), channel_id=1, source_target_pairs={{0,8},{8,16},{16,24},{24,32},{32,40},{40,48},{48,56},{56,64},{64,7... | collective-permute-start | bytes 4616 | tf_op jit(solution)/shard_map/ppermute | solution.py:13
  71.4 12.0 copy-start.21
  72.6 15.4 collective-permute-start.4
  76.1 14.2 collective-permute-start.5
  78.7 52.6 %copy-start.26 = (s32[128]{0:T(128)}, s32[128]{0:T(128)S(1)}, u32[]{:S(2)}) copy-start(s32[128]{0:T(128)S(1)} %reshape.851) | copy-start | bytes 1540
  78.8 54.1 %copy-start.24 = (s32[256]{0:T(256)}, s32[256]{0:T(256)S(1)}, u32[]{:S(2)}) copy-start(s32[256]{0:T(256)S(1)} %reshape.859) | copy-start | bytes 3076
  295.3 15.9 collective-permute-start.6
  300.2 14.6 collective-permute-start.7
  303.1 13.0 collective-permute-start.8
  305.1 12.4 collective-permute-start.9
  309.3 9.5 collective-permute-start.10
  311.2 8.9 collective-permute-start.11
  720.4 15.5 collective-permute-start.12
  725.2 14.3 collective-permute-start.13
  728.3 12.5 collective-permute-start.14
  730.2 11.9 collective-permute-start.15
  734.0 9.5 collective-permute-start.16
  735.9 8.9 collective-permute-start.17
  1145.9 15.4 collective-permute-start.18
  1150.6 14.2 collective-permute-start.19
  1153.7 12.5 collective-permute-start.20
  1155.7 11.8 collective-permute-start.21
  1159.3 9.5 collective-permute-start.22
  1161.3 9.0 collective-permute-start.23
  1171.6 148.6 %copy-start.14 = (f32[8,512]{1,0:T(8,128)S(1)}, f32[8,512]{1,0:T(8,128)}, u32[]{:S(2)}) copy-start(f32[8,512]{1,0:T(8,128)} %constant.4.clone) | copy-start | bytes 49156
  1422.2 100.1 %copy-start.7 = (f32[16]{0:T(128)S(1)}, f32[16]{0:T(128)}, u32[]{:S(2)}) copy-start(f32[16]{0:T(128)} %copy-done.6) | copy-start | bytes 196
  1422.2 100.1 %copy-start.9 = (f32[16]{0:T(128)S(1)}, f32[16]{0:T(128)}, u32[]{:S(2)}) copy-start(f32[16]{0:T(128)} %copy-done.8) | copy-start | bytes 196
  1422.2 100.1 %copy-start.11 = (f32[16]{0:T(128)S(1)}, f32[16]{0:T(128)}, u32[]{:S(2)}) copy-start(f32[16]{0:T(128)} %copy-done.10) | copy-start | bytes 196
  1422.3 100.1 %copy-start.16 = (f32[16]{0:T(128)S(1)}, f32[16]{0:T(128)}, u32[]{:S(2)}) copy-start(f32[16]{0:T(128)} %param.16) | copy-start | bytes 196
  1570.8 15.7 collective-permute-start.24
  1575.5 14.5 collective-permute-start.25
  1578.6 12.8 collective-permute-start.26
  1580.5 12.1 collective-permute-start.27
  1584.3 9.7 collective-permute-start.28
  1586.4 8.9 collective-permute-start.29
  (9 other events, 61.1 us)
where the time goes:
time: 1760 us; the launch traced here: 1750 us
  blocking collectives  1080 us (61%)
  other arithmetic  285 us (16%)
  local copies, waits for them, and re-layouts  279 us (16%)
  starting transfers between devices  78.7 us (4%)
    psum x7, blocking collectives, global_dot(): lax.psum(jnp.sum(left_field * right_field / multiplicity), ('curve', 'spl...  693 us
    psum x4, blocking collectives, precondition(): coarse_image = lax.psum(partial_image, ('curve', 'split'))  390 us
    scatter-add x5, other arithmetic, assemble(): jax.ops.segment_sum(values, point_slots, num_segments=node_count + 1)  218 us
    gather x5, local copies, waits for them, and re-layouts, assemble(): return assembled[:, point_slots].reshape(fields.shape)  210 us
    ppermute x30, starting transfers between devices, from_behind(): return lax.ppermute(block, axis, route)  78.7 us
  transfers between devices with their start and end apart: 30, of which 0 were waited for; matrix products, arithmetic and copies ran while one was open for 3% of the time, Pallas kernels for 0%

commit v1 on v0

--- a/solution.py
+++ b/solution.py
@@ -180,7 +180,7 @@
         scaled = residual_field / multiplicity
         partial_image = coarse_partial(scaled)
         jacobi_part = residual_field / diag_a
-        coarse_image = lax.psum(partial_image, ("curve", "split"))
+        coarse_image = jnp.sum(lax.all_gather(partial_image, ("curve", "split")), axis=0)
         precond_field = jacobi_part + coarse_correction(coarse_image)
         precond_norm = global_dot(residual_field, precond_field)
         return (precond_field, precond_norm)

time: 1760 us -> 2020 us (1.15)
  waiting for transfers between devices: 0.08 us -> 533 us
  blocking collectives: 1080 us -> 692 us
  local copies, waits for them, and re-layouts: 279 us -> 352 us
  other arithmetic: 285 us -> 314 us
    all_gather x0 -> x4, waiting for transfers between devices: none -> 533 us  [precondition(): lax.all_gather(partial_image, ('curve', 'split'))]
    psum x4 -> x0, blocking collectives: 390 us -> none  [precondition(): coarse_image = lax.psum(partial_image, ('curve', 'split'))]
    all_gather x0 -> x4, local copies, waits for them, and re-layouts: none -> 72.9 us  [precondition(): lax.all_gather(partial_image, ('curve', 'split'))]
    reduce_sum x0 -> x4, other arithmetic: none -> 26.2 us  [precondition(): jnp.sum(lax.all_gather(partial_image, ('curve', 'split')), axis=0)]
  transfers between devices with their start and end apart: 30 -> 34, of which waited for: 0 -> 4; matrix products, arithmetic and copies ran while one was open for 3% -> 3% of each run, Pallas kernels for 0% -> 0%
where the time goes in v1:
time: 2020 us; the launch traced here: 2010 us
  blocking collectives  692 us (34%)
  waiting for transfers between devices  533 us (26%)
  local copies, waits for them, and re-layouts  352 us (17%)
  other arithmetic  314 us (16%)
  starting transfers between devices  82.6 us (4%)
  between operations  25 us (1%)
    psum x7, blocking collectives, global_dot(): lax.psum(jnp.sum(left_field * right_field / multiplicity), ('curve', 'spl...  692 us
    all_gather x4, waiting for transfers between devices, precondition(): lax.all_gather(partial_image, ('curve', 'split'))  533 us
    scatter-add x5, other arithmetic, assemble(): jax.ops.segment_sum(values, point_slots, num_segments=node_count + 1)  218 us
    gather x5, local copies, waits for them, and re-layouts, assemble(): return assembled[:, point_slots].reshape(fields.shape)  210 us
    ppermute x30, starting transfers between devices, from_behind(): return lax.ppermute(block, axis, route)  82.4 us
    all_gather x4, local copies, waits for them, and re-layouts, precondition(): lax.all_gather(partial_image, ('curve', 'split'))  72.9 us
  transfers between devices with their start and end apart: 34, of which 4 were waited for; matrix products, arithmetic and copies ran while one was open for 3% of the time, Pallas kernels for 0%

profile of v1, /device:TPU:27, one launch (start us, length us, event | category | flops | bytes accessed | tf_op | source)
XLA Modules:
  0.0 2008.3 jit_solution(11383894770662014076)
XLA Ops:
  17.2 45.0 %scatter_custom_fusion = f32[3,5489]{0,1:T(8,128)S(1)} fusion(s32[8192]{0:T(1024)S(1)} %bitcast.195, f32[8192,3]{1,0:T(8,128)} %copy.20, f32[]{:T(128)} %constant.10.clone.1), kind=kCustom, calls=%fused_computation.89 | custom fusion | flops 24576 | bytes 66380 | tf_op jit(solution)/shard_map/vmap()/scatter-add | solution.py:89
  62.9 4.4 collective-permute-start
  71.2 3.1 collective-permute-start.2
  75.5 3.9 collective-permute-start.3
  100.9 27.7 %gather_fusion.6 = f32[8192,3]{1,0:T(8,128)} fusion(f32[3,5489]{0,1:T(8,128)S(1)} %scatter_custom_fusion.6, s32[8192]{0:T(1024)S(1)} %broadcast_clamp_fusion), kind=kCustom, calls=%fused_computation.6 | custom fusion | bytes 229376 | tf_op jit(solution)/shard_map/gather | solution.py:102
  128.6 10.2 slice_reduce_fusion.1
  140.6 2.9 scatter_custom_fusion.8
  143.8 140.8 %all-gather.9.cloned.1.call-done = f32[4194304]{0:T(1024)} async-done(((f32[8192]{0:T(1024)}), f32[4194304]{0:T(1024)}) %all-gather.9.cloned.1.call-update) | async-done | bytes 16777232 | tf_op jit(solution)/shard_map/all_gather | solution.py:183
  284.7 18.2 reshape.1193
  302.9 6.5 reduce_sum.144
  314.8 43.4 %scatter_custom_fusion.9 = f32[5489]{0:T(1024)S(1)} fusion(s32[8192]{0:T(1024)S(1)} %bitcast.196, f32[8192]{0:T(1024)S(1)} %bitcast.201, f32[]{:T(128)} %constant.10.clone.1), kind=kCustom, calls=%fused_computation.198 | custom fusion | flops 8192 | bytes 21960 | tf_op jit(solution)/shard_map/vmap()/scatter-add | solution.py:89
  363.0 3.4 collective-permute-start.6
  370.6 3.4 collective-permute-start.11
  375.9 4.0 collective-permute-start.9
  389.8 45.5 %gather_fusion.15 = f32[8192]{0:T(1024)S(1)} fusion(f32[5489]{0:T(1024)S(1)} %scatter_fusion.5, s32[8192]{0:T(1024)S(1)} %broadcast_clamp_fusion), kind=kCustom, calls=%fused_computation.15 | custom fusion | bytes 98304 | tf_op jit(solution)/shard_map/gather | solution.py:102
  436.1 99.8 %all-reduce = (f32[]{:T(128)}, f32[]{:T(128)}) all-reduce(f32[]{:T(128)} %get-tuple-element.6, f32[]{:T(128)} %get-tuple-element.5), channel_id=1, replica_groups=mesh['curve'=64,'split'=8] {'curve','split'}, use_global_device_ids=true, to_apply=%region_12.13 | all-reduce | flops 2 | bytes 16 | tf_op jit(solution)/shard_map/psum | solution.py:151
  539.1 3.0 scatter_custom_fusion.17
  542.3 130.6 %all-gather.11.cloned.1.call-done = f32[4194304]{0:T(1024)} async-done(((f32[8192]{0:T(1024)}), f32[4194304]{0:T(1024)}) %all-gather.11.cloned.1.call-update) | async-done | bytes 16777232 | tf_op jit(solution)/shard_map/all_gather | solution.py:183
  672.9 18.2 reshape.1194
  691.1 6.5 reduce_sum.148
  701.6 97.5 %psum.58 = f32[]{:T(128)} all-reduce(f32[]{:T(128)} %get-tuple-element.18), channel_id=1, replica_groups=mesh['curve'=64,'split'=8] {'curve','split'}, use_global_device_ids=true, to_apply=%region_27.28 | all-reduce | flops 1 | bytes 8 | tf_op jit(solution)/shard_map/psum | solution.py:151
  802.1 43.2 %scatter_custom_fusion.18 = f32[5489]{0:T(1024)S(1)} fusion(s32[8192]{0:T(1024)S(1)} %bitcast.197, f32[8192]{0:T(1024)S(1)} %bitcast.202, f32[]{:T(128)} %constant.10.clone.1), kind=kCustom, calls=%fused_computation.196 | custom fusion | flops 8192 | bytes 21960 | tf_op jit(solution)/shard_map/vmap()/scatter-add | solution.py:89
  850.5 3.2 collective-permute-start.12
  860.1 3.4 collective-permute-start.14
  863.5 2.9 collective-permute-start.15
  876.7 45.5 %gather_fusion.24 = f32[8192]{0:T(1024)S(1)} fusion(f32[5489]{0:T(1024)S(1)} %scatter_fusion.11, s32[8192]{0:T(1024)S(1)} %broadcast_clamp_fusion), kind=kCustom, calls=%fused_computation.24 | custom fusion | bytes 98304 | tf_op jit(solution)/shard_map/gather | solution.py:102
  922.8 100.2 %psum.59 = f32[]{:T(128)} all-reduce(f32[]{:T(128)} %fusion.33), channel_id=1, replica_groups=mesh['curve'=64,'split'=8] {'curve','split'}, use_global_device_ids=true, to_apply=%region_36.37 | all-reduce | flops 1 | bytes 8 | tf_op jit(solution)/shard_map/psum | solution.py:151
  1027.4 3.0 scatter_custom_fusion.26
  1030.5 130.6 %all-gather.13.cloned.1.call-done = f32[4194304]{0:T(1024)} async-done(((f32[8192]{0:T(1024)}), f32[4194304]{0:T(1024)}) %all-gather.13.cloned.1.call-update) | async-done | bytes 16777232 | tf_op jit(solution)/shard_map/all_gather | solution.py:183
  1161.1 18.2 reshape.1195
  1179.3 6.5 reduce_sum.152
  1189.9 97.3 %psum.60 = f32[]{:T(128)} all-reduce(f32[]{:T(128)} %get-tuple-element.20), channel_id=1, replica_groups=mesh['curve'=64,'split'=8] {'curve','split'}, use_global_device_ids=true, to_apply=%region_42.43 | all-reduce | flops 1 | bytes 8 | tf_op jit(solution)/shard_map/psum | solution.py:151
  1290.2 43.2 %scatter_custom_fusion.27 = f32[5489]{0:T(1024)S(1)} fusion(s32[8192]{0:T(1024)S(1)} %bitcast.198, f32[8192]{0:T(1024)S(1)} %bitcast.203, f32[]{:T(128)} %constant.10.clone.1), kind=kCustom, calls=%fused_computation.194 | custom fusion | flops 8192 | bytes 21960 | tf_op jit(solution)/shard_map/vmap()/scatter-add | solution.py:89
  1338.6 3.2 collective-permute-start.18
  1348.3 3.4 collective-permute-start.20
  1365.1 45.5 %gather_fusion.33 = f32[8192]{0:T(1024)S(1)} fusion(f32[5489]{0:T(1024)S(1)} %scatter_fusion.17, s32[8192]{0:T(1024)S(1)} %broadcast_clamp_fusion), kind=kCustom, calls=%fused_computation.33 | custom fusion | bytes 98304 | tf_op jit(solution)/shard_map/gather | solution.py:102
  1411.2 100.2 %psum.61 = f32[]{:T(128)} all-reduce(f32[]{:T(128)} %fusion.35), channel_id=1, replica_groups=mesh['curve'=64,'split'=8] {'curve','split'}, use_global_device_ids=true, to_apply=%region_51.52 | all-reduce | flops 1 | bytes 8 | tf_op jit(solution)/shard_map/psum | solution.py:151
  1514.7 3.0 scatter_custom_fusion.35
  1517.7 130.7 %all-gather.15.cloned.1.call-done = f32[4194304]{0:T(1024)} async-done(((f32[8192]{0:T(1024)}), f32[4194304]{0:T(1024)}) %all-gather.15.cloned.1.call-update) | async-done | bytes 16777232 | tf_op jit(solution)/shard_map/all_gather | solution.py:183
  1648.4 18.2 reshape.1196
  1666.6 6.5 reduce_sum.156
  1677.2 97.3 %psum.62 = f32[]{:T(128)} all-reduce(f32[]{:T(128)} %get-tuple-element.22), channel_id=1, replica_groups=mesh['curve'=64,'split'=8] {'curve','split'}, use_global_device_ids=true, to_apply=%region_57.58 | all-reduce | flops 1 | bytes 8 | tf_op jit(solution)/shard_map/psum | solution.py:151
  1777.6 43.2 %scatter_custom_fusion.36 = f32[5489]{0:T(1024)S(1)} fusion(s32[8192]{0:T(1024)S(1)} %bitcast.199, f32[8192]{0:T(1024)S(1)} %bitcast.200, f32[]{:T(128)} %constant.10.clone.1), kind=kCustom, calls=%fused_computation.192 | custom fusion | flops 8192 | bytes 21960 | tf_op jit(solution)/shard_map/vmap()/scatter-add | solution.py:89
  1825.9 3.4 collective-permute-start.24
  1838.6 2.9 collective-permute-start.27
  1841.6 3.6 collective-permute-start.29
  1853.1 45.5 %gather_fusion.42 = f32[8192]{0:T(1024)S(1)} fusion(f32[5489]{0:T(1024)S(1)} %scatter_fusion.23, s32[8192]{0:T(1024)S(1)} %broadcast_clamp_fusion), kind=kCustom, calls=%fused_computation.42 | custom fusion | bytes 98304 | tf_op jit(solution)/shard_map/gather | solution.py:102
  1899.2 99.8 %psum.63 = f32[]{:T(128)} all-reduce(f32[]{:T(128)} %fusion.37), channel_id=1, replica_groups=mesh['curve'=64,'split'=8] {'curve','split'}, use_global_device_ids=true, to_apply=%region_66.67 | all-reduce | flops 1 | bytes 8 | tf_op jit(solution)/shard_map/psum | solution.py:151
  (297 shorter events, 161.2 us)
Async XLA Ops:
  7.2 277.5 %all-gather.9.cloned.1.call-start = ((), (), s32[]{:S(2)}) async-start(), calls=%async_computation | async-start | bytes 16809984 | tf_op jit(solution)/shard_map/all_gather | solution.py:183
  8.8 1281.3 %copy-start.13 = (f32[16]{0:T(128)}, f32[16]{0:T(128)S(1)}, u32[]{:S(2)}) copy-start(f32[16]{0:T(128)S(1)} %get-tuple-element.13) | copy-start | bytes 196
  8.8 1281.3 %copy-start.15 = (f32[16]{0:T(128)}, f32[16]{0:T(128)S(1)}, u32[]{:S(2)}) copy-start(f32[16]{0:T(128)S(1)} %get-tuple-element.14) | copy-start | bytes 196
  8.8 1281.3 %copy-start.17 = (f32[16]{0:T(128)}, f32[16]{0:T(128)S(1)}, u32[]{:S(2)}) copy-start(f32[16]{0:T(128)S(1)} %get-tuple-element.15) | copy-start | bytes 196
  17.2 344.6 %copy-start.27 = (s32[1024]{0:T(1024)}, s32[1024]{0:T(1024)S(1)}, u32[]{:S(2)}) copy-start(s32[1024]{0:T(1024)S(1)} %get-tuple-element.27) | copy-start | bytes 12292
  17.2 836.5 %copy-start.26 = (s32[1024]{0:T(1024)}, s32[1024]{0:T(1024)S(1)}, u32[]{:S(2)}) copy-start(s32[1024]{0:T(1024)S(1)} %get-tuple-element.26) | copy-start | bytes 12292
  62.9 21.1 %collective-permute-start = (f32[3,128]{0,1:T(8,128)S(1)}, f32[3,128]{0,1:T(8,128)S(1)}, u32[]{:S(2)}, u32[]{:S(2)}) collective-permute-start(f32[3,128]{0,1:T(8,128)S(1)} %bitcast.253), channel_id=1, source_target_pairs={{0,1},{1,2},{2,3},{3,4},{4,5},{5,6},{6,7},{8,9},{9,10},{10,11},{11... | collective-permute-start | bytes 4616 | tf_op jit(solution)/shard_map/ppermute | solution.py:13
  67.9 21.0 %collective-permute-start.1 = (f32[3,128]{0,1:T(8,128)S(1)}, f32[3,128]{0,1:T(8,128)S(1)}, u32[]{:S(2)}, u32[]{:S(2)}) collective-permute-start(f32[3,128]{0,1:T(8,128)S(1)} %bitcast.252), channel_id=1, source_target_pairs={{1,0},{2,1},{3,2},{4,3},{5,4},{6,5},{7,6},{9,8},{10,9},{11,10},{12... | collective-permute-start | bytes 4616 | tf_op jit(solution)/shard_map/ppermute | solution.py:13
  69.9 801.5 %copy-start.10 = (s32[128]{0:T(128)}, s32[128]{0:T(128)S(1)}, u32[]{:S(2)}) copy-start(s32[128]{0:T(128)S(1)} %get-tuple-element.11) | copy-start | bytes 1540
  69.9 802.8 %copy-start.8 = (s32[128]{0:T(128)}, s32[128]{0:T(128)S(1)}, u32[]{:S(2)}) copy-start(s32[128]{0:T(128)S(1)} %get-tuple-element.12) | copy-start | bytes 1540
  69.9 804.2 %copy-start.6 = (s32[128]{0:T(128)}, s32[128]{0:T(128)S(1)}, u32[]{:S(2)}) copy-start(s32[128]{0:T(128)S(1)} %get-tuple-element.9) | copy-start | bytes 1540
  69.9 289.5 %copy-start.29 = (s32[1024]{0:T(1024)}, s32[1024]{0:T(1024)S(1)}, u32[]{:S(2)}) copy-start(s32[1024]{0:T(1024)S(1)} %get-tuple-element.30) | copy-start | bytes 12292
  69.9 290.7 %copy-start.28 = (s32[1024]{0:T(1024)}, s32[1024]{0:T(1024)S(1)}, u32[]{:S(2)}) copy-start(s32[1024]{0:T(1024)S(1)} %get-tuple-element.31) | copy-start | bytes 12292
  71.2 20.1 %collective-permute-start.2 = (f32[3,128]{0,1:T(8,128)}, f32[3,128]{0,1:T(8,128)S(1)}, u32[]{:S(2)}, u32[]{:S(2)}) collective-permute-start(f32[3,128]{0,1:T(8,128)} %bitcast.16), channel_id=1, source_target_pairs={{0,16},{8,24},{16,32},{24,40},{32,48},{40,56},{48,64},{56,72},{64,... | collective-permute-start | bytes 4616 | tf_op jit(solution)/shard_map/ppermute | solution.py:13
  75.5 18.1 collective-permute-start.3
  79.5 288.0 %copy-start.30 = (s32[1024]{0:T(1024)}, s32[1024]{0:T(1024)S(1)}, u32[]{:S(2)}) copy-start(s32[1024]{0:T(1024)S(1)} %get-tuple-element.28) | copy-start | bytes 12292
  80.7 15.1 collective-permute-start.4
  84.0 14.2 collective-permute-start.5
  143.6 529.3 %all-gather.11.cloned.1.call-start = ((), (), s32[]{:S(2)}) async-start(), calls=%async_computation.1 | async-start | bytes 16809984 | tf_op jit(solution)/shard_map/all_gather | solution.py:183
  363.0 17.0 collective-permute-start.6
  368.7 14.5 collective-permute-start.7
  370.6 17.9 collective-permute-start.11
  374.0 10.6 collective-permute-start.8
  375.9 9.9 collective-permute-start.9
  380.0 7.2 collective-permute-start.10
  542.2 618.9 %all-gather.13.cloned.1.call-start = ((), (), s32[]{:S(2)}) async-start(), calls=%async_computation.2 | async-start | bytes 16809984 | tf_op jit(solution)/shard_map/all_gather | solution.py:183
  850.5 15.9 collective-permute-start.12
  856.1 13.9 collective-permute-start.13
  858.2 17.2 collective-permute-start.17
  860.1 11.3 collective-permute-start.14
  863.5 9.2 collective-permute-start.15
  866.4 7.6 collective-permute-start.16
  1030.4 618.0 %all-gather.15.cloned.1.call-start = ((), (), s32[]{:S(2)}) async-start(), calls=%async_computation.3 | async-start | bytes 16809984 | tf_op jit(solution)/shard_map/all_gather | solution.py:183
  1338.6 16.1 collective-permute-start.18
  1344.3 13.9 collective-permute-start.19
  1346.4 17.3 collective-permute-start.23
  1348.3 11.3 collective-permute-start.20
  1351.7 9.2 collective-permute-start.21
  1354.6 7.6 collective-permute-start.22
  1365.1 147.7 %copy-start.22 = (f32[8,512]{1,0:T(8,128)S(1)}, f32[8,512]{1,0:T(8,128)}, u32[]{:S(2)}) copy-start(f32[8,512]{1,0:T(8,128)} %constant.4.clone) | copy-start | bytes 49156
  1676.3 101.2 %copy-start.14 = (f32[16]{0:T(128)S(1)}, f32[16]{0:T(128)}, u32[]{:S(2)}) copy-start(f32[16]{0:T(128)} %copy-done.13) | copy-start | bytes 196
  1676.3 101.2 %copy-start.16 = (f32[16]{0:T(128)S(1)}, f32[16]{0:T(128)}, u32[]{:S(2)}) copy-start(f32[16]{0:T(128)} %copy-done.15) | copy-start | bytes 196
  1825.9 15.7 collective-permute-start.24
  1831.9 14.5 collective-permute-start.25
  1834.0 16.5 collective-permute-start.28
  1836.7 11.1 collective-permute-start.26
  1838.6 10.5 collective-permute-start.27
  1841.6 10.2 collective-permute-start.29
  (21 other events, 824.6 us)
Sparse Core Ops, SparseCore 0:
  143.7 140.9 all-gather.8
  542.3 130.4 all-gather.10
  1030.6 130.5 all-gather.12
  1517.9 130.5 all-gather.14
